TPU v7x, 256 devices: a whole 4x4x8 slice. The times are simulated.
256 devices in a mesh: blk: 32 (over x, z), leaf: 4 (over y), samp: 2 (over core).
Axes of the slice: x: 4, y: 4, z: 8, core: 2. Of those that a mesh axis runs over, the one named last changes fastest.
Arguments:
- points: float32 [3, 32768], P(None, ('blk', 'leaf')), may hold values from 0 to 64, as said below
- neighbors: int32 [128, 8], P(('blk', 'leaf')), may hold values from -1 to 127, as said below
- omega: float32 [512, 32768], P(None, ('blk', 'leaf')), may hold values from -6 to 6
- observed: float32 [32768], P(('blk', 'leaf')), may hold values from -6 to 6
- prior_draws: float32 [64, 32768], P('samp', ('blk', 'leaf')), may hold values from -6 to 6
Outputs:
- weights: float32 [64, 32768], P('samp', ('blk', 'leaf'))
- residual: float32 [64, 32768], P('samp', ('blk', 'leaf'))
Inputs may be any that keep to these rules, and one draw needn't show every extreme that they name: Block g's points lie in the unit cell with integer corner (cx, cy, cz), where cx // 2 = g // 4 and 0 <= cy, cz < 3. `neighbors`: row g lists in ascending order every block h whose unit cell touches g's (cells at most one apart in every coordinate, the first taken periodic of period 2 * 32), which includes every block with a point within distance 1 of a point of g, followed by -1 in the unused slots; the relation is symmetric, and every listed block has a slab index h // 4 equal to or cyclically next to g // 4.
All inputs are finite; a program needn't handle non-finite values.
Results may differ from a plain program's by a relative error of at most 0.0003.
Values sent between devices are 32-bit elements; how exact they have to be, the bound alone decides.
A program may use at most 64 MiB of HBM per device.

v0:
```python
import jax
import jax.numpy as jnp
from jax import lax
from jax.sharding import PartitionSpec as P

PB = 256
ITERS = 2
support_radius = 0.8
noise_variance = 1.0
sketch_shift = 1.0
ALL_AXES = ("blk", "leaf", "samp")


def shifted_2(block, axis, distance):
    devices = range(lax.axis_size(axis))
    route = [((i - distance) % len(devices), i) for i in devices]
    return lax.ppermute(block, axis, route)


def wendland(row_points, column_points, period):
    offset = row_points[None, :, :, None] - column_points[:, :, None, :]
    half_period = 0.5 * period
    along_x = jnp.mod(offset[:, 0] + half_period, period) - half_period
    squared = along_x * along_x + offset[:, 1] * offset[:, 1] + offset[:, 2] * offset[:, 2]
    radius = jnp.sqrt(squared) / support_radius
    remain = jnp.maximum(1.0 - radius, 0.0)
    return remain**4 * (4.0 * radius + 1.0)


def high_dot(left, right):
    return jnp.dot(left, right, precision=lax.Precision.HIGHEST, preferred_element_type=jnp.float32)


def shifted(values, offset_by):
    return shifted_2(values, "blk", offset_by)


def beside_all(values):
    slab_values = lax.all_gather(values, "leaf", axis=1, tiled=True)
    return jnp.concatenate([shifted(slab_values, 1), slab_values, shifted(slab_values, -1)], axis=1)


def lower_solve(factor, values):
    return lax.linalg.triangular_solve(factor, values, left_side=True, lower=True)


def local(points, neighbors, omega, observed, prior_draws):
    blk_dev = neighbors.shape[0]
    cycle_count = lax.axis_size("blk")
    slab_blocks = blk_dev * lax.axis_size("leaf")
    period = 2.0 * cycle_count
    own_slab = lax.axis_index("blk")
    n_samp = lax.axis_size("samp")
    samp_idx = lax.axis_index("samp")
    usable = neighbors >= 0
    relative = jnp.mod(neighbors // slab_blocks - own_slab + 1, cycle_count)
    chosen = jnp.where(usable, relative * slab_blocks + jnp.mod(neighbors, slab_blocks), 0)
    usable_weight = usable.astype(jnp.float32)
    reach_points = beside_all(points)
    reach_blocks = reach_points.reshape(3, 3 * slab_blocks, PB).transpose(1, 0, 2)
    row_blocks = points.reshape(3, blk_dev, PB).transpose(1, 0, 2)
    kernel_tile = wendland(row_blocks[0], reach_blocks[chosen[0]], period)
    kernel_tile = kernel_tile * usable_weight[0][:, None, None]

    def apply_kernel(values):
        width = values.shape[0]
        reach = beside_all(values).reshape(width, 3 * slab_blocks, PB)
        picked = jnp.take(reach, chosen[0], axis=1)
        return jnp.einsum("cnj,nij->ci", picked, kernel_tile, precision=lax.Precision.HIGHEST)

    def slot(x):
        zeros = jnp.zeros((n_samp,) + x.shape, x.dtype)
        return lax.dynamic_update_index_in_dim(zeros, x, samp_idx, 0)

    def unslot(xs):
        return lax.dynamic_index_in_dim(xs, samp_idx, 0, keepdims=False)

    def total_per_samp(values):
        return jax.tree.map(unslot, lax.psum(jax.tree.map(slot, values), ALL_AXES))

    sketch = apply_kernel(omega) + sketch_shift * omega
    rhs = observed[None, :] - prior_draws
    half = PB // n_samp
    omega_half = lax.dynamic_slice_in_dim(omega, samp_idx * half, half, axis=1)
    sketch_half = lax.dynamic_slice_in_dim(sketch, samp_idx * half, half, axis=1)
    core_part = high_dot(omega_half, sketch_half.T)
    square_part = high_dot(sketch_half, sketch_half.T)
    joint_part = 0.5 * (core_part + core_part.T) + 0.5 * (square_part + square_part.T)
    rhs_part = slot(high_dot(sketch, rhs.T))
    joint_gram, rhs_proj = lax.psum((joint_part, rhs_part), ALL_AXES)
    rhs_proj = unslot(rhs_proj)
    joint_factor = jnp.linalg.cholesky(joint_gram)

    def precond_from(vectors, projected):
        first_solve = lower_solve(joint_factor, projected)
        solved = lax.linalg.triangular_solve(
            joint_factor, first_solve, left_side=True, lower=True, transpose_a=True
        )
        return (vectors - high_dot(solved.T, sketch)) / noise_variance

    residual = rhs
    projected = rhs_proj
    precond = precond_from(residual, projected)
    direction = precond
    weights = jnp.zeros_like(rhs)
    image = apply_kernel(direction) + noise_variance * direction
    inner_now, curvature, image_proj = total_per_samp(
        (
            jnp.sum(residual * precond, axis=1),
            jnp.sum(direction * image, axis=1),
            high_dot(sketch, image.T),
        )
    )
    step_size = inner_now / curvature
    weights = weights + step_size[:, None] * direction
    residual = residual - step_size[:, None] * image
    projected = projected - step_size[None, :] * image_proj
    precond = precond_from(residual, projected)
    inner_next = total_per_samp(jnp.sum(residual * precond, axis=1))
    direction = precond + (inner_next / inner_now)[:, None] * direction
    inner_now = inner_next
    image = apply_kernel(direction) + noise_variance * direction
    curvature = total_per_samp(jnp.sum(direction * image, axis=1))
    step_size = inner_now / curvature
    weights = weights + step_size[:, None] * direction
    residual = residual - step_size[:, None] * image
    return (weights, residual)


def solution(mesh):
    in_specs = (
        P(None, ("blk", "leaf")),
        P(("blk", "leaf"), None),
        P(None, ("blk", "leaf")),
        P(("blk", "leaf")),
        P("samp", ("blk", "leaf")),
    )
    out_specs = (P("samp", ("blk", "leaf")), P("samp", ("blk", "leaf")))
    return jax.shard_map(local, mesh=mesh, in_specs=in_specs, out_specs=out_specs, check_vma=False)
```

profile of v0, /device:TPU:1, one launch (start us, length us, event | category | flops | bytes accessed | tf_op | source)
XLA Modules:
  0.0 1005.4 jit_solution(9335899095662480256)
XLA Ops:
  9.3 10.5 %all_gather.13 = f32[3,1024]{1,0:T(4,128)S(1)} all-gather(f32[3,256]{1,0:T(4,128)} %param.11), channel_id=1, replica_groups=mesh['blk'=32,'leaf'=4,'samp'=2] {'leaf'}, dimensions={1}, use_global_device_ids=true | all-gather | bytes 15360 | tf_op jit(solution)/shard_map/all_gather | solution.py:39
  19.9 7.8 collective-permute-start.3
  27.6 19.4 %all-gather.2.cloned.1.call-done = f32[512,1024]{0,1:T(8,128)} async-done(((f32[512,256]{0,1:T(8,128)}), f32[512,1024]{0,1:T(8,128)}) %all-gather.2.cloned.1.call-update) | async-done | bytes 2097168 | tf_op jit(solution)/shard_map/all_gather | solution.py:39
  47.1 5.2 collective-permute-start.1
  55.7 2.6 multiply_multiply_fusion
  58.3 38.5 %collective-permute-done.1 = f32[512,1024]{0,1:T(8,128)} collective-permute-done((f32[512,1024]{0,1:T(8,128)}, f32[512,1024]{0,1:T(8,128)}, u32[]{:S(2)}, u32[]{:S(2)}) %collective-permute-start.1) | collective-permute-done | bytes 2097184 | tf_op jit(solution)/shard_map/ppermute | solution.py:17
  96.8 5.4 collective-permute-done
  102.2 5.6 pad_maximum_fusion
  107.8 6.5 copy.11
  114.3 5.6 gather_fusion
  119.9 5.5 fusion.17
  134.5 3.7 fusion.26
  139.7 250.3 %all-reduce.8.cloned.1.call-done = (f32[512,512]{1,0:T(8,128)}, f32[2,512,32]{1,2,0:T(8,128)}) async-done(((f32[512,512]{1,0:T(8,128)}, f32[2,512,32]{1,2,0:T(8,128)}), (f32[512,512]{1,0:T(8,128)}, f32[2,512,32]{1,2,0:T(8,128)})) %all-reduce.8.cloned.1.call-update) | async-done | bytes 1179664 | tf_op jit(solution)/shard_map/psum | solution.py:90
  396.2 11.7 %cholesky.104 = f32[128,128]{1,0:T(8,128)S(1)} custom-call(f32[128,128]{1,0:T(8,128)S(1)} %cholesky.266), custom_call_target="Cholesky" | custom-call | tf_op jit(solution)/shard_map/jit(cholesky)/cholesky | solution.py:92
  407.9 9.8 custom-call.33
  422.1 11.7 %cholesky.217 = f32[128,128]{1,0:T(8,128)S(1)} custom-call(f32[128,128]{1,0:T(8,128)S(1)} %cholesky.270), custom_call_target="Cholesky" | custom-call | tf_op jit(solution)/shard_map/jit(cholesky)/cholesky | solution.py:92
  434.5 10.2 %custom-call.34 = f32[1,128,128]{1,2,0:T(8,128)S(1)} custom-call(f32[1,128,128]{2,1,0:T(8,128)S(1)} %get-tuple-element.61), custom_call_target="InvertDiagBlocksLowerTriangular" | custom-call | tf_op jit(solution)/shard_map/jit(cholesky)/cholesky | solution.py:92
  447.1 11.7 %cholesky.238 = f32[128,128]{1,0:T(8,128)S(1)} custom-call(f32[128,128]{1,0:T(8,128)S(1)} %cholesky.275), custom_call_target="Cholesky" | custom-call | tf_op jit(solution)/shard_map/jit(cholesky)/cholesky | solution.py:92
  460.2 9.8 custom-call.35
  472.3 11.7 %cholesky.255 = f32[128,128]{1,0:T(8,128)S(1)} custom-call(f32[128,128]{1,0:T(8,128)S(1)} %convolution_subtract_fusion.2), custom_call_target="Cholesky" | custom-call | tf_op jit(solution)/shard_map/jit(cholesky)/cholesky | solution.py:92
  491.1 12.0 %while.8 = (s32[]{:T(128)}, f32[512,512]{1,0:T(8,128)}, s32[4,2]{0,1:T(2,128)S(1)}, f32[4,128,128]{2,1,0:T(8,128)S(1)}, s32[]{:T(128)}) while((s32[]{:T(128)}, f32[512,512]{1,0:T(8,128)}, s32[4,2]{0,1:T(2,128)S(1)}, f32[4,128,128]{2,1,0:T(8,128)S(1)}, s32[]{:T(128)}) %tuple.51), condition=%wide.while_cond.1, body=%wide.while_body.1.sunk | while | flops 2 | bytes 131189 | solution.py:96
  503.1 39.3 %custom-call.39 = f32[4,128,128]{1,2,0:T(8,128)S(1)} custom-call(f32[4,128,128]{2,1,0:T(8,128)S(1)} %get-tuple-element.34), custom_call_target="InvertDiagBlocksLowerTriangular" | custom-call | tf_op jit(solution)/shard_map/triangular_solve/custom-call.8 | solution.py:96
  551.2 9.2 all_gather.14
  560.4 5.0 collective-permute-start.5
  567.4 5.2 collective-permute-done.4
  573.2 2.8 multiply_reduce_fusion.3
  577.5 76.1 %all-reduce.1 = (f32[2,32]{1,0:T(2,128)S(1)}, f32[2,32]{1,0:T(2,128)S(1)}) all-reduce(f32[2,32]{1,0:T(2,128)S(1)} %dynamic_update_slice.22, f32[2,32]{1,0:T(2,128)S(1)} %dynamic_update_slice.21), channel_id=1, replica_groups=mesh['blk'=32,'leaf'=4,'samp'=2] {'blk','leaf','samp'}, use_global_device_ids=true, to_apply=%region_13.17 | all-reduce | flops 128 | bytes 1024 | tf_op jit(solution)/shard_map/psum | solution.py:79
  653.7 161.9 %all-reduce.6.cloned.1.call-done = f32[2,512,32]{1,2,0:T(8,128)} async-done(((f32[2,512,32]{1,2,0:T(8,128)}), f32[2,512,32]{1,2,0:T(8,128)}) %all-reduce.6.cloned.1.call-update) | async-done | bytes 131088 | tf_op jit(solution)/shard_map/psum | solution.py:79
  825.4 75.9 %psum.54 = f32[2,32]{1,0:T(2,128)S(1)} all-reduce(f32[2,32]{1,0:T(2,128)S(1)} %dynamic_update_slice.24), channel_id=1, replica_groups=mesh['blk'=32,'leaf'=4,'samp'=2] {'blk','leaf','samp'}, use_global_device_ids=true, to_apply=%region_16.20 | all-reduce | flops 64 | bytes 512 | tf_op jit(solution)/shard_map/psum | solution.py:79
  901.4 9.1 all_gather.15
  914.5 4.6 collective-permute-done.6
  921.8 76.2 %psum.55 = f32[2,32]{1,0:T(2,128)S(1)} all-reduce(f32[2,32]{1,0:T(2,128)S(1)} %dynamic_update_slice.25), channel_id=1, replica_groups=mesh['blk'=32,'leaf'=4,'samp'=2] {'blk','leaf','samp'}, use_global_device_ids=true, to_apply=%region_18.22 | all-reduce | flops 64 | bytes 512 | tf_op jit(solution)/shard_map/psum | solution.py:79
  (144 shorter events, 79.6 us)
Async XLA Ops:
  7.2 39.9 %all-gather.2.cloned.1.call-start = ((), (), s32[]{:S(2)}) async-start(), calls=%async_computation | async-start | bytes 2621440 | tf_op jit(solution)/shard_map/all_gather | solution.py:39
  9.3 380.7 %all-reduce.8.cloned.1.call-start = ((), (), s32[]{:S(2)}) async-start(), calls=%async_computation.2 | async-start | bytes 2359296 | tf_op jit(solution)/shard_map/psum | solution.py:90
  19.9 33.9 %collective-permute-start.3 = (f32[3,1024]{1,0:T(4,128)S(1)}, f32[3,1024]{1,0:T(4,128)S(1)}, u32[]{:S(2)}, u32[]{:S(2)}) collective-permute-start(f32[3,1024]{1,0:T(4,128)S(1)} %all_gather.13), channel_id=1, source_target_pairs={{8,0},{16,8},{24,16},{32,24},{40,32},{48,40},{56,48},{64,56},{72,6... | collective-permute-start | bytes 36872 | tf_op jit(solution)/shard_map/ppermute | solution.py:17
  27.6 26.1 %collective-permute-start.2 = (f32[3,1024]{1,0:T(4,128)S(1)}, f32[3,1024]{1,0:T(4,128)S(1)}, u32[]{:S(2)}, u32[]{:S(2)}) collective-permute-start(f32[3,1024]{1,0:T(4,128)S(1)} %all_gather.13), channel_id=1, source_target_pairs={{248,0},{0,8},{8,16},{16,24},{24,32},{32,40},{40,48},{48,56},{56,6... | collective-permute-start | bytes 36872 | tf_op jit(solution)/shard_map/ppermute | solution.py:17
  47.1 49.8 %collective-permute-start.1 = (f32[512,1024]{0,1:T(8,128)}, f32[512,1024]{0,1:T(8,128)}, u32[]{:S(2)}, u32[]{:S(2)}) collective-permute-start(f32[512,1024]{0,1:T(8,128)} %all-gather.2.cloned.1.call-done), channel_id=1, source_target_pairs={{8,0},{16,8},{24,16},{32,24},{40,32},{48,40},{56,48},{64,56},{72,6... | collective-permute-start | bytes 6291464 | tf_op jit(solution)/shard_map/ppermute | solution.py:17
  52.2 50.0 %collective-permute-start = (f32[512,1024]{0,1:T(8,128)}, f32[512,1024]{0,1:T(8,128)}, u32[]{:S(2)}, u32[]{:S(2)}) collective-permute-start(f32[512,1024]{0,1:T(8,128)} %all-gather.2.cloned.1.call-done), channel_id=1, source_target_pairs={{248,0},{0,8},{8,16},{16,24},{24,32},{32,40},{40,48},{48,56},{56,6... | collective-permute-start | bytes 6291464 | tf_op jit(solution)/shard_map/ppermute | solution.py:17
  55.7 46.5 %copy-start.2 = (f32[512,1024]{0,1:T(8,128)S(1)}, f32[512,1024]{0,1:T(8,128)}, u32[]{:S(2)}) copy-start(f32[512,1024]{0,1:T(8,128)} %all-gather.2.cloned.1.call-done) | copy-start | bytes 6291460
  114.3 5.6 copy-start
  134.5 3.7 copy-start.5
  134.5 3.7 copy-start.10
  138.8 0.6 copy-start.7
  139.4 676.2 %all-reduce.6.cloned.1.call-start = ((), (), s32[]{:S(2)}) async-start(), calls=%async_computation.1 | async-start | bytes 262144 | tf_op jit(solution)/shard_map/psum | solution.py:79
  395.2 1.0 copy-start.1
  551.2 16.2 %copy-start.3 = (f32[32,256]{1,0:T(8,128)}, f32[32,256]{1,0:T(8,128)S(1)}, u32[]{:S(2)}) copy-start(f32[32,256]{1,0:T(8,128)S(1)} %convolution_subtract_fusion.4) | copy-start | bytes 98308
  560.4 7.0 collective-permute-start.5
  565.4 7.1 collective-permute-start.4
  573.2 80.4 %copy-start.6 = (f32[32,256]{1,0:T(8,128)S(1)}, f32[32,256]{1,0:T(8,128)}, u32[]{:S(2)}) copy-start(f32[32,256]{1,0:T(8,128)} %param.15) | copy-start | bytes 98308
  573.2 242.4 %copy-start.9 = (f32[2,512,32]{1,2,0:T(8,128)S(1)}, f32[2,512,32]{1,2,0:T(8,128)}, u32[]{:S(2)}) copy-start(f32[2,512,32]{1,2,0:T(8,128)} %get-tuple-element.50) | copy-start | bytes 393220
  576.1 325.3 %copy-start.4 = (f32[32,256]{1,0:T(8,128)S(1)}, f32[32,256]{1,0:T(8,128)}, u32[]{:S(2)}) copy-start(f32[32,256]{1,0:T(8,128)} %copy-done.3) | copy-start | bytes 98308
  576.7 0.7 copy-start.8
  910.5 4.0 collective-permute-start.7
  911.9 7.1 collective-permute-start.6
Sparse Core Ops, SparseCore 0:
  9.8 37.2 all-gather.1
  139.5 250.3 all-reduce.7
  577.5 238.0 all-reduce.5
where the time goes:
time: 1010 us
  waiting for transfers between devices  490 us (49%)
  blocking collectives  257 us (25%)
  other arithmetic  141 us (14%)
  matrix products  40.6 us (4%)
  local copies, waits for them, and re-layouts  40.1 us (4%)
  starting transfers between devices  20.1 us (2%)
  between operations  17.2 us (2%)
    psum x1, waiting for transfers between devices, local(): joint_gram, rhs_proj = lax.psum((joint_part, rhs_part), ALL_AXES)  250 us
    psum x3, blocking collectives, total_per_samp(): return jax.tree.map(unslot, lax.psum(jax.tree.map(slot, values), ALL_AXES))  228 us
    psum x1, waiting for transfers between devices, total_per_samp(): return jax.tree.map(unslot, lax.psum(jax.tree.map(slot, values), ALL_AXES))  162 us
    another operation x14, other arithmetic, local(): joint_factor = jnp.linalg.cholesky(joint_gram)  80.7 us
    ppermute x8, waiting for transfers between devices, shifted_2(): return lax.ppermute(block, axis, route)  57.9 us
    another operation x4, other arithmetic, precond_from(): lax.linalg.triangular_solve(joint_factor, first_solve, left_side=True, lo...  41.8 us
    all_gather x3, blocking collectives, beside_all(): slab_values = lax.all_gather(values, 'leaf', axis=1, tiled=True)  28.8 us
  transfers between devices with their start and end apart: 11, of which 9 were waited for; matrix products, arithmetic and copies ran while one was open for 1% of the time, Pallas kernels for 0%

commit v1 on v0

--- a/solution.py
+++ b/solution.py
@@ -87,7 +87,7 @@
     square_part = high_dot(sketch_half, sketch_half.T)
     joint_part = 0.5 * (core_part + core_part.T) + 0.5 * (square_part + square_part.T)
     rhs_part = slot(high_dot(sketch, rhs.T))
-    joint_gram, rhs_proj = lax.psum((joint_part, rhs_part), ALL_AXES)
+    joint_gram, rhs_proj = lax.psum(lax.psum((joint_part, rhs_part), "blk"), ("leaf", "samp"))
     rhs_proj = unslot(rhs_proj)
     joint_factor = jnp.linalg.cholesky(joint_gram)
 

time: 1010 us -> 971 us (0.961)
  waiting for transfers between devices: 490 us -> 449 us
    psum x1 -> x2, waiting for transfers between devices: 250 us -> 210 us  [the longest x1 139 us: local(): lax.psum((joint_part, rhs_part), 'blk')]
  transfers between devices with their start and end apart: 11 -> 12, of which waited for: 9 -> 10; matrix products, arithmetic and copies ran while one was open for 1% -> 1% of each run, Pallas kernels for 0% -> 0%
where the time goes in v1:
time: 971 us; the launch traced here: 967 us
  waiting for transfers between devices  449 us (46%)
  blocking collectives  259 us (27%)
  other arithmetic  141 us (15%)
  matrix products  40.6 us (4%)
  local copies, waits for them, and re-layouts  40 us (4%)
  starting transfers between devices  20.3 us (2%)
  between operations  17.2 us (2%)
    psum x3, blocking collectives, total_per_samp(): return jax.tree.map(unslot, lax.psum(jax.tree.map(slot, values), ALL_AXES))  229 us
    psum x1, waiting for transfers between devices, total_per_samp(): return jax.tree.map(unslot, lax.psum(jax.tree.map(slot, values), ALL_AXES))  162 us
    psum x1, waiting for transfers between devices, local(): lax.psum((joint_part, rhs_part), 'blk')  139 us
    another operation x14, other arithmetic, local(): joint_factor = jnp.linalg.cholesky(joint_gram)  80.7 us
    psum x1, waiting for transfers between devices, local(): lax.psum(lax.psum((joint_part, rhs_part), 'blk'), ('leaf', 'samp'))  70.2 us
    ppermute x8, waiting for transfers between devices, shifted_2(): return lax.ppermute(block, axis, route)  57.9 us
    another operation x4, other arithmetic, precond_from(): lax.linalg.triangular_solve(joint_factor, first_solve, left_side=True, lo...  41.8 us
    all_gather x3, blocking collectives, beside_all(): slab_values = lax.all_gather(values, 'leaf', axis=1, tiled=True)  29.6 us
  transfers between devices with their start and end apart: 12, of which 10 were waited for; matrix products, arithmetic and copies ran while one was open for 1% of the time, Pallas kernels for 0%

profile of v1, /device:TPU:1, one launch (start us, length us, event | category | flops | bytes accessed | tf_op | source)
XLA Modules:
  0.0 966.7 jit_solution(11207303951882600330)
XLA Ops:
  9.3 10.5 %all_gather.13 = f32[3,1024]{1,0:T(4,128)S(1)} all-gather(f32[3,256]{1,0:T(4,128)} %param.11), channel_id=1, replica_groups=mesh['blk'=32,'leaf'=4,'samp'=2] {'leaf'}, dimensions={1}, use_global_device_ids=true | all-gather | bytes 15360 | tf_op jit(solution)/shard_map/all_gather | solution.py:39
  19.9 7.8 collective-permute-start.3
  27.6 19.4 %all-gather.2.cloned.1.call-done = f32[512,1024]{0,1:T(8,128)} async-done(((f32[512,256]{0,1:T(8,128)}), f32[512,1024]{0,1:T(8,128)}) %all-gather.2.cloned.1.call-update) | async-done | bytes 2097168 | tf_op jit(solution)/shard_map/all_gather | solution.py:39
  47.1 5.2 collective-permute-start.1
  58.3 38.5 %collective-permute-done.1 = f32[512,1024]{0,1:T(8,128)} collective-permute-done((f32[512,1024]{0,1:T(8,128)}, f32[512,1024]{0,1:T(8,128)}, u32[]{:S(2)}, u32[]{:S(2)}) %collective-permute-start.1) | collective-permute-done | bytes 2097184 | tf_op jit(solution)/shard_map/ppermute | solution.py:17
  96.8 5.4 collective-permute-done
  102.2 5.6 pad_maximum_fusion
  107.8 6.5 copy.11
  114.3 5.6 gather_fusion
  119.9 5.5 fusion.17
  134.5 3.7 fusion.26
  139.5 139.4 %all-reduce.10.cloned.1.call-done = (f32[512,512]{1,0:T(8,128)}, f32[2,512,32]{1,2,0:T(8,128)}) async-done(((f32[512,512]{1,0:T(8,128)}, f32[2,512,32]{1,2,0:T(8,128)}), (f32[512,512]{1,0:T(8,128)}, f32[2,512,32]{1,2,0:T(8,128)})) %all-reduce.10.cloned.1.call-update) | async-done | bytes 1179664 | tf_op jit(solution)/shard_map/psum | solution.py:90
  279.2 70.2 %all-reduce.12.cloned.1.call-done = (f32[512,512]{1,0:T(8,128)}, f32[2,512,32]{1,2,0:T(8,128)}) async-done(((f32[512,512]{1,0:T(8,128)}, f32[2,512,32]{1,2,0:T(8,128)}), (f32[512,512]{1,0:T(8,128)}, f32[2,512,32]{1,2,0:T(8,128)})) %all-reduce.12.cloned.1.call-update) | async-done | bytes 1179664 | tf_op jit(solution)/shard_map/psum | solution.py:90
  355.5 11.7 %cholesky.104 = f32[128,128]{1,0:T(8,128)S(1)} custom-call(f32[128,128]{1,0:T(8,128)S(1)} %cholesky.266), custom_call_target="Cholesky" | custom-call | tf_op jit(solution)/shard_map/jit(cholesky)/cholesky | solution.py:92
  367.3 9.8 %custom-call.33 = f32[1,128,128]{1,2,0:T(8,128)S(1)} custom-call(f32[1,128,128]{2,1,0:T(8,128)S(1)} %get-tuple-element.66), custom_call_target="InvertDiagBlocksLowerTriangular" | custom-call | tf_op jit(solution)/shard_map/jit(cholesky)/cholesky | solution.py:92
  381.5 11.7 %cholesky.217 = f32[128,128]{1,0:T(8,128)S(1)} custom-call(f32[128,128]{1,0:T(8,128)S(1)} %cholesky.270), custom_call_target="Cholesky" | custom-call | tf_op jit(solution)/shard_map/jit(cholesky)/cholesky | solution.py:92
  393.9 10.2 %custom-call.34 = f32[1,128,128]{1,2,0:T(8,128)S(1)} custom-call(f32[1,128,128]{2,1,0:T(8,128)S(1)} %get-tuple-element.63), custom_call_target="InvertDiagBlocksLowerTriangular" | custom-call | tf_op jit(solution)/shard_map/jit(cholesky)/cholesky | solution.py:92
  406.5 11.7 %cholesky.238 = f32[128,128]{1,0:T(8,128)S(1)} custom-call(f32[128,128]{1,0:T(8,128)S(1)} %cholesky.275), custom_call_target="Cholesky" | custom-call | tf_op jit(solution)/shard_map/jit(cholesky)/cholesky | solution.py:92
  419.6 9.8 %custom-call.35 = f32[1,128,128]{1,2,0:T(8,128)S(1)} custom-call(f32[1,128,128]{2,1,0:T(8,128)S(1)} %get-tuple-element.60), custom_call_target="InvertDiagBlocksLowerTriangular" | custom-call | tf_op jit(solution)/shard_map/jit(cholesky)/cholesky | solution.py:92
  431.6 11.7 %cholesky.255 = f32[128,128]{1,0:T(8,128)S(1)} custom-call(f32[128,128]{1,0:T(8,128)S(1)} %convolution_subtract_fusion.2), custom_call_target="Cholesky" | custom-call | tf_op jit(solution)/shard_map/jit(cholesky)/cholesky | solution.py:92
  450.4 12.0 %while.8 = (s32[]{:T(128)}, f32[512,512]{1,0:T(8,128)}, s32[4,2]{0,1:T(2,128)S(1)}, f32[4,128,128]{2,1,0:T(8,128)S(1)}, s32[]{:T(128)}) while((s32[]{:T(128)}, f32[512,512]{1,0:T(8,128)}, s32[4,2]{0,1:T(2,128)S(1)}, f32[4,128,128]{2,1,0:T(8,128)S(1)}, s32[]{:T(128)}) %tuple.51), condition=%wide.while_cond.1, body=%wide.while_body.1.sunk | while | flops 2 | bytes 131189 | solution.py:96
  462.5 39.3 %custom-call.39 = f32[4,128,128]{1,2,0:T(8,128)S(1)} custom-call(f32[4,128,128]{2,1,0:T(8,128)S(1)} %get-tuple-element.34), custom_call_target="InvertDiagBlocksLowerTriangular" | custom-call | tf_op jit(solution)/shard_map/triangular_solve/custom-call.8 | solution.py:96
  510.5 10.0 %all_gather.14 = f32[32,1024]{1,0:T(8,128)S(1)} all-gather(f32[32,256]{1,0:T(8,128)S(1)} %convolution_subtract_fusion.4), channel_id=1, replica_groups=mesh['blk'=32,'leaf'=4,'samp'=2] {'leaf'}, dimensions={1}, use_global_device_ids=true | all-gather | bytes 163840 | tf_op jit(solution)/shard_map/all_gather | solution.py:39
  520.6 5.2 collective-permute-start.5
  527.7 5.2 collective-permute-done.4
  533.5 2.8 multiply_reduce_fusion.3
  537.8 77.2 %all-reduce.1 = (f32[2,32]{1,0:T(2,128)S(1)}, f32[2,32]{1,0:T(2,128)S(1)}) all-reduce(f32[2,32]{1,0:T(2,128)S(1)} %dynamic_update_slice.22, f32[2,32]{1,0:T(2,128)S(1)} %dynamic_update_slice.21), channel_id=1, replica_groups=mesh['blk'=32,'leaf'=4,'samp'=2] {'blk','leaf','samp'}, use_global_device_ids=true, to_apply=%region_15.19 | all-reduce | flops 128 | bytes 1024 | tf_op jit(solution)/shard_map/psum | solution.py:79
  615.0 161.8 %all-reduce.8.cloned.1.call-done = f32[2,512,32]{1,2,0:T(8,128)} async-done(((f32[2,512,32]{1,2,0:T(8,128)}), f32[2,512,32]{1,2,0:T(8,128)}) %all-reduce.8.cloned.1.call-update) | async-done | bytes 131088 | tf_op jit(solution)/shard_map/psum | solution.py:79
  786.7 75.9 %psum.70 = f32[2,32]{1,0:T(2,128)S(1)} all-reduce(f32[2,32]{1,0:T(2,128)S(1)} %dynamic_update_slice.24), channel_id=1, replica_groups=mesh['blk'=32,'leaf'=4,'samp'=2] {'blk','leaf','samp'}, use_global_device_ids=true, to_apply=%region_18.22 | all-reduce | flops 64 | bytes 512 | tf_op jit(solution)/shard_map/psum | solution.py:79
  862.7 9.1 all_gather.15
  875.8 4.6 collective-permute-done.6
  883.1 76.2 %psum.71 = f32[2,32]{1,0:T(2,128)S(1)} all-reduce(f32[2,32]{1,0:T(2,128)S(1)} %dynamic_update_slice.25), channel_id=1, replica_groups=mesh['blk'=32,'leaf'=4,'samp'=2] {'blk','leaf','samp'}, use_global_device_ids=true, to_apply=%region_20.24 | all-reduce | flops 64 | bytes 512 | tf_op jit(solution)/shard_map/psum | solution.py:79
  (145 shorter events, 82.3 us)
Async XLA Ops:
  7.2 39.9 %all-gather.2.cloned.1.call-start = ((), (), s32[]{:S(2)}) async-start(), calls=%async_computation | async-start | bytes 2621440 | tf_op jit(solution)/shard_map/all_gather | solution.py:39
  9.3 269.6 %all-reduce.10.cloned.1.call-start = ((), (), s32[]{:S(2)}) async-start(), calls=%async_computation.2 | async-start | bytes 2359296 | tf_op jit(solution)/shard_map/psum | solution.py:90
  19.9 33.9 %collective-permute-start.3 = (f32[3,1024]{1,0:T(4,128)S(1)}, f32[3,1024]{1,0:T(4,128)S(1)}, u32[]{:S(2)}, u32[]{:S(2)}) collective-permute-start(f32[3,1024]{1,0:T(4,128)S(1)} %all_gather.13), channel_id=1, source_target_pairs={{8,0},{16,8},{24,16},{32,24},{40,32},{48,40},{56,48},{64,56},{72,6... | collective-permute-start | bytes 36872 | tf_op jit(solution)/shard_map/ppermute | solution.py:17
  27.6 26.1 %collective-permute-start.2 = (f32[3,1024]{1,0:T(4,128)S(1)}, f32[3,1024]{1,0:T(4,128)S(1)}, u32[]{:S(2)}, u32[]{:S(2)}) collective-permute-start(f32[3,1024]{1,0:T(4,128)S(1)} %all_gather.13), channel_id=1, source_target_pairs={{248,0},{0,8},{8,16},{16,24},{24,32},{32,40},{40,48},{48,56},{56,6... | collective-permute-start | bytes 36872 | tf_op jit(solution)/shard_map/ppermute | solution.py:17
  47.1 49.8 %collective-permute-start.1 = (f32[512,1024]{0,1:T(8,128)}, f32[512,1024]{0,1:T(8,128)}, u32[]{:S(2)}, u32[]{:S(2)}) collective-permute-start(f32[512,1024]{0,1:T(8,128)} %all-gather.2.cloned.1.call-done), channel_id=1, source_target_pairs={{8,0},{16,8},{24,16},{32,24},{40,32},{48,40},{56,48},{64,56},{72,6... | collective-permute-start | bytes 6291464 | tf_op jit(solution)/shard_map/ppermute | solution.py:17
  52.2 50.0 %collective-permute-start = (f32[512,1024]{0,1:T(8,128)}, f32[512,1024]{0,1:T(8,128)}, u32[]{:S(2)}, u32[]{:S(2)}) collective-permute-start(f32[512,1024]{0,1:T(8,128)} %all-gather.2.cloned.1.call-done), channel_id=1, source_target_pairs={{248,0},{0,8},{8,16},{16,24},{24,32},{32,40},{40,48},{48,56},{56,6... | collective-permute-start | bytes 6291464 | tf_op jit(solution)/shard_map/ppermute | solution.py:17
  55.7 46.5 %copy-start.2 = (f32[512,1024]{0,1:T(8,128)S(1)}, f32[512,1024]{0,1:T(8,128)}, u32[]{:S(2)}) copy-start(f32[512,1024]{0,1:T(8,128)} %all-gather.2.cloned.1.call-done) | copy-start | bytes 6291460
  114.3 5.6 copy-start
  134.5 3.7 copy-start.5
  134.5 3.7 copy-start.9
  138.8 0.6 copy-start.7
  139.4 210.0 %all-reduce.12.cloned.1.call-start = ((), (), s32[]{:S(2)}) async-start(), calls=%async_computation.3 | async-start | bytes 2359296 | tf_op jit(solution)/shard_map/psum | solution.py:90
  278.9 498.0 %all-reduce.8.cloned.1.call-start = ((), (), s32[]{:S(2)}) async-start(), calls=%async_computation.1 | async-start | bytes 262144 | tf_op jit(solution)/shard_map/psum | solution.py:79
  354.5 1.0 copy-start.1
  510.5 17.2 %copy-start.3 = (f32[32,256]{1,0:T(8,128)}, f32[32,256]{1,0:T(8,128)S(1)}, u32[]{:S(2)}) copy-start(f32[32,256]{1,0:T(8,128)S(1)} %convolution_subtract_fusion.4) | copy-start | bytes 98308
  520.6 7.1 collective-permute-start.5
  525.7 7.1 collective-permute-start.4
  533.5 81.4 %copy-start.6 = (f32[32,256]{1,0:T(8,128)S(1)}, f32[32,256]{1,0:T(8,128)}, u32[]{:S(2)}) copy-start(f32[32,256]{1,0:T(8,128)} %param.15) | copy-start | bytes 98308
  536.4 326.3 %copy-start.4 = (f32[32,256]{1,0:T(8,128)S(1)}, f32[32,256]{1,0:T(8,128)}, u32[]{:S(2)}) copy-start(f32[32,256]{1,0:T(8,128)} %copy-done.3) | copy-start | bytes 98308
  537.0 0.7 copy-start.8
  871.8 4.0 collective-permute-start.7
  873.2 7.1 collective-permute-start.6
Sparse Core Ops, SparseCore 0:
  9.8 37.2 all-gather.1
  139.5 139.2 all-reduce.9
  281.3 67.9 all-reduce.11
  537.8 239.0 all-reduce.7
